TPU v7x, 512 devices: a whole 4x4x16 slice. The times are simulated.
512 devices in a mesh: cell: 128 (over z, x, core), lag: 4 (over y).
Axes of the slice: x: 4, y: 4, z: 16, core: 2. Of those that a mesh axis runs over, the one named last changes fastest.
Arguments:
- green: bfloat16 [32, 640, 32768], P('lag', None, 'cell'), may hold values from -0.0078125 to 0.0078125
- source: bfloat16 [8, 48, 32768], P(None, None, 'cell'), may hold values from -6 to 6
- observed: float32 [8, 48, 640], replicated, may hold values from -6 to 6
- lag_gaps: int32 [31], replicated, may hold values from 1 to 2, 47 in all
- huber_level: int32 [640], replicated, may hold values from 0 to 7
Outputs:
- gradient: float32 [8, 48, 32768], P(None, 'lag', 'cell')
Inputs may be any that keep to these rules, and one draw needn't show every extreme that they name: `lag_gaps`: the gaps sum to 47.
All inputs are finite; a program needn't handle non-finite values.
Results may differ from a plain program's by a relative error of at most 0.0034.
Values may be sent and summed in bfloat16 or wider, within the bound.
No kernel may reach another device: no remote copies, remote signals or barrier semaphores. Data moves between devices by JAX's collectives and lax.ppermute only.
A program may use at most 64 MiB of HBM per device.

v0:
```python
import jax
import jax.numpy as jnp
from jax import lax
from jax.sharding import PartitionSpec as P


def body(green, source, observed, lag_gaps, huber_level):
    rows, steps, cells = source.shape
    sensors = green.shape[1]
    own_count = green.shape[0]
    lag_table = jnp.concatenate([jnp.zeros((1,), jnp.int32), jnp.cumsum(lag_gaps)])
    first = lax.axis_index("lag") * own_count
    lag_of = lax.dynamic_slice_in_dim(lag_table, first, own_count, 0)
    padded = jnp.concatenate([jnp.zeros_like(source), source], axis=1)
    predicted = jnp.zeros((rows, steps, sensors), jnp.float32)
    for block in range(own_count):
        shifted = lax.dynamic_slice_in_dim(padded, steps - lag_of[block], steps, 1)
        predicted = predicted + jnp.einsum(
            "rtc,sc->rts", shifted, green[block], preferred_element_type=jnp.float32
        )
    threshold = 0.3 * (huber_level.astype(jnp.float32) + 1.0)
    summed = lax.psum(predicted, ("cell", "lag"))
    misfit = summed - observed
    weighted = (misfit * threshold / jnp.maximum(jnp.abs(misfit), threshold)).astype(jnp.bfloat16)
    later = jnp.concatenate([weighted, jnp.zeros_like(weighted)], axis=1)
    terms = jnp.zeros((rows, steps, cells), jnp.float32)
    for block in range(own_count):
        window = lax.dynamic_slice_in_dim(later, lag_of[block], steps, 1)
        terms = terms + jnp.einsum(
            "rts,sc->rtc", window, green[block], preferred_element_type=jnp.float32
        )
    return lax.psum_scatter(terms, "lag", scatter_dimension=1, tiled=True)


def solution(mesh):
    in_specs = (P("lag", None, "cell"), P(None, None, "cell"), P(), P(), P())
    out_specs = P(None, "lag", "cell")
    return jax.shard_map(body, mesh=mesh, in_specs=in_specs, out_specs=out_specs, check_vma=False)
```

profile of v0, /device:TPU:2, one launch (start us, length us, event | category | flops | bytes accessed | tf_op | source)
XLA Modules:
  0.0 551.9 jit_solution(6812498945430603760)
XLA Ops:
  6.5 0.0 all-reduce.4.cloned.1.call-start
  6.5 0.9 copy.10
  7.4 0.1 reduce-window.9
  7.5 0.1 reduce
  7.6 0.1 pad_add_fusion
  7.7 0.1 dynamic_slice.51
  7.8 0.7 fusion.66
  18.6 1.4 fusion.16
  20.0 2.4 convolution_add_fusion.6
  22.5 0.0 copy-done.1
  22.5 0.0 copy-done
  22.5 2.5 convolution_add_fusion.5
  25.0 2.5 convolution_add_fusion.4
  27.6 2.5 convolution_add_fusion.3
  30.1 2.5 convolution_add_fusion.2
  32.6 2.6 convolution_add_fusion.1
  35.2 2.5 convolution_add_fusion
  37.8 0.0 all-reduce.4.cloned.1.call-update
  37.8 0.0 reduce-scatter.2.cloned.1.call-start
  53.0 459.9 %all-reduce.4.cloned.1.call-done = f32[8,48,640]{2,1,0:T(8,128)} async-done(((f32[8,48,640]{2,1,0:T(8,128)}), f32[8,48,640]{2,1,0:T(8,128)}) %all-reduce.4.cloned.1.call-update) | async-done | bytes 983056 | tf_op jit(solution)/shard_map/psum | solution.py:22
  512.9 1.7 divide_convert_fusion
  514.6 0.3 fusion
  515.0 0.3 convolution_add_fusion.13
  515.3 0.3 convolution_add_fusion.12
  515.7 0.3 convolution_add_fusion.11
  516.0 0.3 convolution_add_fusion.10
  516.4 0.3 convolution_add_fusion.9
  516.7 0.3 convolution_add_fusion.8
  517.1 0.3 convolution_add_fusion.7
  517.4 1.0 copy.11
  518.4 0.0 reduce-scatter.2.cloned.1.call-update
  518.4 26.7 %reduce-scatter.2.cloned.1.call-done = f32[8,12,256]{2,0,1:T(8,128)} async-done(((f32[8,48,256]{2,0,1:T(8,128)}), f32[8,12,256]{2,0,1:T(8,128)}) %reduce-scatter.2.cloned.1.call-update) | async-done | bytes 98320 | tf_op jit(solution)/shard_map/reduce_scatter | solution.py:32
  (5 shorter events, 0.0 us)
Async XLA Ops:
  6.5 15.9 %copy-start.1 = (bf16[8,640,256]{2,1,0:T(8,128)(2,1)S(1)}, bf16[8,640,256]{2,1,0:T(8,128)(2,1)}, u32[]{:S(2)}) copy-start(bf16[8,640,256]{2,1,0:T(8,128)(2,1)} %param.5) | copy-start | bytes 7864324
  6.5 15.9 %copy-start = (bf16[8,48,256]{2,1,0:T(8,128)(2,1)S(1)}, bf16[8,48,256]{2,1,0:T(8,128)(2,1)}, u32[]{:S(2)}) copy-start(bf16[8,48,256]{2,1,0:T(8,128)(2,1)} %param.6) | copy-start | bytes 589828
  6.5 506.4 %all-reduce.4.cloned.1.call-start = ((), (), s32[]{:S(2)}) async-start(), calls=%async_computation.1 | async-start | bytes 1966080 | tf_op jit(solution)/shard_map/psum | solution.py:22
  32.6 20.3 %copy-start.2 = (s32[640]{0:T(1024)S(1)}, s32[640]{0:T(1024)}, u32[]{:S(2)}) copy-start(s32[640]{0:T(1024)} %param.9) | copy-start | bytes 7684
  37.8 507.3 %reduce-scatter.2.cloned.1.call-start = ((), (), s32[]{:S(2)}) async-start(), calls=%async_computation.2 | async-start | bytes 491520 | tf_op jit(solution)/shard_map/reduce_scatter | solution.py:32
Sparse Core Ops, SparseCore 0:
  37.9 474.9 all-reduce.3
  518.5 26.5 reduce-scatter.1
where the time goes:
time: 553 us; the launch traced here: 552 us
  waiting for transfers between devices  487 us (88%)
  between operations  38.8 us (7%)
  matrix products  21.9 us (4%)
    psum x1, waiting for transfers between devices, body(): summed = lax.psum(predicted, ('cell', 'lag'))  460 us
    reduce_scatter x1, waiting for transfers between devices, body(): return lax.psum_scatter(terms, 'lag', scatter_dimension=1, tiled=True)  26.7 us
    dot_general x8, matrix products, body(): jnp.einsum('rtc,sc->rts', shifted, green[block], preferred_element_type=j...  19.1 us
  transfers between devices with their start and end apart: 2, of which 2 were waited for; matrix products, arithmetic and copies ran while one was open for 0% of the time, Pallas kernels for 0%

commit v1 on v0

--- a/solution.py
+++ b/solution.py
@@ -19,7 +19,7 @@
             "rtc,sc->rts", shifted, green[block], preferred_element_type=jnp.float32
         )
     threshold = 0.3 * (huber_level.astype(jnp.float32) + 1.0)
-    summed = lax.psum(predicted, ("cell", "lag"))
+    summed = lax.psum(lax.psum(predicted, "cell"), "lag")
     misfit = summed - observed
     weighted = (misfit * threshold / jnp.maximum(jnp.abs(misfit), threshold)).astype(jnp.bfloat16)
     later = jnp.concatenate([weighted, jnp.zeros_like(weighted)], axis=1)

time: 553 us -> 491 us (0.89)
  the two profiles are of different devices: /device:TPU:2 before, /device:TPU:4 now
where the time goes in v1:
time: 491 us; the launch traced here: 490 us
  waiting for transfers between devices  425 us (87%)
  between operations  38.5 us (8%)
  matrix products  21.9 us (4%)
    psum x2, waiting for transfers between devices, body(): summed = lax.psum(lax.psum(predicted, 'cell'), 'lag')  395 us
    reduce_scatter x1, waiting for transfers between devices, body(): return lax.psum_scatter(terms, 'lag', scatter_dimension=1, tiled=True)  30.1 us
    dot_general x8, matrix products, body(): jnp.einsum('rtc,sc->rts', shifted, green[block], preferred_element_type=j...  19.2 us
  transfers between devices with their start and end apart: 3, of which 3 were waited for; matrix products, arithmetic and copies ran while one was open for 0% of the time, Pallas kernels for 0%

profile of v1, /device:TPU:4, one launch (start us, length us, event | category | flops | bytes accessed | tf_op | source)
XLA Modules:
  0.0 490.0 jit_solution(1034769991848796646)
XLA Ops:
  6.5 0.9 copy.10
  7.4 0.1 reduce-window.9
  7.5 0.1 reduce
  7.6 0.1 pad_add_fusion
  7.7 0.1 dynamic_slice.51
  7.8 0.7 fusion.66
  18.6 1.4 fusion.16
  20.0 2.4 convolution_add_fusion.6
  22.5 2.5 convolution_add_fusion.5
  25.0 2.5 convolution_add_fusion.4
  27.6 2.5 convolution_add_fusion.3
  30.1 2.5 convolution_add_fusion.2
  32.6 2.5 convolution_add_fusion.1
  35.2 2.6 convolution_add_fusion
  37.8 0.0 all-reduce.5.cloned.1.call-update
  37.8 0.0 all-reduce.7.cloned.1.call-start
  37.8 347.8 %all-reduce.5.cloned.1.call-done = f32[8,48,640]{2,1,0:T(8,128)} async-done(((f32[8,48,640]{2,1,0:T(8,128)}), f32[8,48,640]{2,1,0:T(8,128)}) %all-reduce.5.cloned.1.call-update) | async-done | bytes 983056 | tf_op jit(solution)/shard_map/psum | solution.py:22
  385.7 0.0 all-reduce.7.cloned.1.call-update
  385.7 0.0 reduce-scatter.2.cloned.1.call-start
  400.9 47.0 %all-reduce.7.cloned.1.call-done = f32[8,48,640]{2,1,0:T(8,128)} async-done(((f32[8,48,640]{2,1,0:T(8,128)}), f32[8,48,640]{2,1,0:T(8,128)}) %all-reduce.7.cloned.1.call-update) | async-done | bytes 983056 | tf_op jit(solution)/shard_map/psum | solution.py:22
  447.9 1.7 divide_convert_fusion
  449.6 0.3 fusion
  450.0 0.3 convolution_add_fusion.13
  450.4 0.3 convolution_add_fusion.12
  450.7 0.3 convolution_add_fusion.11
  451.1 0.3 convolution_add_fusion.10
  451.4 0.3 convolution_add_fusion.9
  451.8 0.3 convolution_add_fusion.8
  452.1 0.3 convolution_add_fusion.7
  452.4 1.0 copy.11
  453.4 0.0 reduce-scatter.2.cloned.1.call-update
  453.4 30.1 %reduce-scatter.2.cloned.1.call-done = f32[8,12,256]{2,0,1:T(8,128)} async-done(((f32[8,48,256]{2,0,1:T(8,128)}), f32[8,12,256]{2,0,1:T(8,128)}) %reduce-scatter.2.cloned.1.call-update) | async-done | bytes 98320 | tf_op jit(solution)/shard_map/reduce_scatter | solution.py:32
  (8 shorter events, 0.0 us)
Async XLA Ops:
  6.5 15.9 %copy-start.1 = (bf16[8,640,256]{2,1,0:T(8,128)(2,1)S(1)}, bf16[8,640,256]{2,1,0:T(8,128)(2,1)}, u32[]{:S(2)}) copy-start(bf16[8,640,256]{2,1,0:T(8,128)(2,1)} %param.5) | copy-start | bytes 7864324
  6.5 15.9 %copy-start = (bf16[8,48,256]{2,1,0:T(8,128)(2,1)S(1)}, bf16[8,48,256]{2,1,0:T(8,128)(2,1)}, u32[]{:S(2)}) copy-start(bf16[8,48,256]{2,1,0:T(8,128)(2,1)} %param.6) | copy-start | bytes 589828
  6.5 379.1 %all-reduce.5.cloned.1.call-start = ((), (), s32[]{:S(2)}) async-start(), calls=%async_computation.1 | async-start | bytes 1966080 | tf_op jit(solution)/shard_map/psum | solution.py:22
  35.2 365.7 %copy-start.2 = (s32[640]{0:T(1024)S(1)}, s32[640]{0:T(1024)}, u32[]{:S(2)}) copy-start(s32[640]{0:T(1024)} %param.9) | copy-start | bytes 7684
  37.8 410.2 %all-reduce.7.cloned.1.call-start = ((), (), s32[]{:S(2)}) async-start(), calls=%async_computation.2 | async-start | bytes 1966080 | tf_op jit(solution)/shard_map/psum | solution.py:22
  385.7 97.8 %reduce-scatter.2.cloned.1.call-start = ((), (), s32[]{:S(2)}) async-start(), calls=%async_computation.3 | async-start | bytes 491520 | tf_op jit(solution)/shard_map/reduce_scatter | solution.py:32
Sparse Core Ops, SparseCore 0:
  37.9 347.7 all-reduce.4
  388.1 59.8 all-reduce.6
  453.6 29.9 reduce-scatter.1
